TPU v7x, 128 devices: a whole 4x4x4 slice. The times are simulated.
128 devices in a mesh: row: 16 (over z, x), col: 8 (over y, core).
Axes of the slice: x: 4, y: 4, z: 4, core: 2. Of those that a mesh axis runs over, the one named last changes fastest.
Arguments:
- child_front: bfloat16 [16, 4096, 1024], P('row', 'col'), may hold values from -6 to 6
- child_inverse: bfloat16 [16, 1024, 1024], P('row'), as said below
- child_index: int32 [16, 32], P('row'), may hold values from 0 to 79, as said below
- child_size: int32 [16], P('row'), may hold values from 4 to 32, as said below
- front: float32 [10240, 10240], P('row', 'col'), may hold values from -6 to 6
- panel_inverse: float32 [256, 256], replicated, as said below
Outputs:
- trailing: float32 [10240, 10240], P('row', 'col')
- panel_rows: float32 [10240, 256], P('row')
Inputs may be any that keep to these rules, and one draw needn't show every extreme that they name: `child_index`: for each child r, the entries t < child_size[r] are increasing root tile numbers; later entries are arbitrary tile numbers and are not used. Cutting the root tiles into aligned runs of 5 tiles, a child has at most 2 live tiles in any run, and exactly 2 in each of two neighbouring runs 2q and 2q + 1 for some q. `child_size`: some child has the smallest and some child the largest possible size in every draw. `child_inverse`: lower triangular with a positive diagonal. `panel_inverse`: lower triangular with a positive diagonal.
All inputs are finite; a program needn't handle non-finite values.
Results may differ from a plain program's by a relative error of at most 0.0034.
Values may be sent and summed in bfloat16 or wider, within the bound.
A program may use at most 128 MiB of HBM per device.

v0:
```python
import jax
import jax.numpy as jnp
from jax import lax
from jax.sharding import PartitionSpec as P

TILE = 128
PANEL = 256
BLOCK_TILES = 2


def from_root(value, axis, source):
    kept = jnp.where(lax.axis_index(axis) == source, value, 0).astype(value.dtype)
    return lax.psum(kept, axis)


def slot_tiles(tile_index, first_slot, slot_count, slot_width, base_tile, sentinel):
    positions = jnp.arange(slot_width, dtype=jnp.int32)
    picked = jnp.take(tile_index, jnp.clip(first_slot + positions, 0, tile_index.shape[0] - 1))
    return jnp.where(positions < slot_count, picked - base_tile, sentinel)


def shards(child_front, child_inverse, child_index, child_size, front, panel_inverse):
    precise = lax.Precision.HIGHEST
    rows_dev = front.shape[0]
    cols_dev = front.shape[1]
    tiles_row = rows_dev // TILE
    tiles_col = cols_dev // TILE
    blocks = lax.axis_size("row")
    column = lax.axis_index("col")
    double = 2 * BLOCK_TILES
    factor_part = lax.dot_general(
        child_front[0],
        child_inverse[0],
        (((1,), (1,)), ((), ())),
        preferred_element_type=jnp.float32,
    ).astype(jnp.bfloat16)
    factor = lax.all_gather(factor_part, "col", axis=0, tiled=True)
    tile_index = child_index[0]
    live_tiles = jnp.arange(tile_index.shape[0], dtype=jnp.int32) < child_size[0]
    row_owner = jnp.where(live_tiles, tile_index // tiles_row, blocks)
    targets = jnp.arange(blocks, dtype=jnp.int32)
    starts = jnp.sum((row_owner[None, :] < targets[:, None]).astype(jnp.int32), axis=1)
    counts = jnp.sum((row_owner[None, :] == targets[:, None]).astype(jnp.int32), axis=1)
    col_owner = jnp.where(live_tiles, tile_index // tiles_col, lax.axis_size("col"))
    col_start = jnp.sum((col_owner < column).astype(jnp.int32))
    col_count = jnp.sum((col_owner == column).astype(jnp.int32))
    padded = jnp.concatenate(
        [factor, jnp.zeros((double * TILE, factor.shape[1]), factor.dtype)], axis=0
    )

    def row_rows(first_tile):
        return lax.dynamic_slice_in_dim(padded, first_tile * TILE, BLOCK_TILES * TILE, 0)

    def row_slots(first_tile, tile_count, target):
        return slot_tiles(
            tile_index, first_tile, tile_count, BLOCK_TILES, target * tiles_row, tiles_row
        )

    row_parts = jax.vmap(row_rows)(starts)
    col_part = lax.dynamic_slice_in_dim(padded, col_start * TILE, double * TILE, 0)
    row_targets = jax.vmap(row_slots)(starts, counts, targets)
    col_targets = slot_tiles(
        tile_index, col_start, col_count, double, column * tiles_col, tiles_col
    )
    col_sent = jnp.broadcast_to(col_targets[None, :], (blocks, double))
    width = padded.shape[1]
    row_tiles = row_parts.reshape(blocks, BLOCK_TILES, TILE, width)
    col_tiles = col_part.reshape(double, TILE, width)
    contribution = -jnp.einsum(
        "ikap,jbp->ikjab", row_tiles, col_tiles, preferred_element_type=jnp.float32
    )
    arrived, arrived_rows, arrived_cols = (
        lax.all_to_all(contribution, "row", split_axis=0, concat_axis=0, tiled=True),
        lax.all_to_all(row_targets, "row", split_axis=0, concat_axis=0, tiled=True),
        lax.all_to_all(col_sent, "row", split_axis=0, concat_axis=0, tiled=True),
    )
    tiled = front.reshape(tiles_row, TILE, tiles_col, TILE)
    tiled = tiled.at[arrived_rows[:, :, None], :, arrived_cols[:, None, :], :].add(
        arrived, mode="drop"
    )
    assembled = tiled.reshape(rows_dev, cols_dev)
    own_panel = lax.dot_general(
        assembled[:, :PANEL], panel_inverse, (((1,), (1,)), ((), ())), precision=precise
    )
    panel_rows = from_root(own_panel, "col", 0)
    whole_panel = lax.all_gather(panel_rows, "row", axis=0, tiled=True)
    across = lax.dynamic_slice_in_dim(whole_panel, column * cols_dev, cols_dev, 0)
    trailing = assembled - lax.dot_general(
        panel_rows, across, (((1,), (1,)), ((), ())), precision=precise
    )
    return (trailing, panel_rows)


def solution(mesh):
    in_specs = (
        P("row", "col", None),
        P("row", None, None),
        P("row", None),
        P("row"),
        P("row", "col"),
        P(),
    )
    out_specs = (P("row", "col"), P("row", None))
    return jax.shard_map(shards, mesh=mesh, in_specs=in_specs, out_specs=out_specs, check_vma=False)
```

profile of v0, /device:TPU:1, one launch (start us, length us, event | category | flops | bytes accessed | tf_op | source)
XLA Modules:
  0.0 468.3 jit_solution(3586415045492164564)
XLA Ops:
  8.8 3.5 fusion.2
  14.7 8.4 %all-to-all-start = ((s32[16,1,2]{2,1,0:T(1,128)}), s32[16,1,2]{2,1,0:T(1,128)S(1)}, u32[]{:S(2)}, u32[]{:S(2)}) async-start(s32[16,1,2]{2,1,0:T(1,128)} %bitcast.3), calls=%async_computation | async-start | bytes 16384 | tf_op jit(solution)/shard_map/all_to_all | solution.py:74
  27.2 38.6 %all-gather.3.cloned.1.call-done = bf16[4096,1024]{1,0:T(8,128)(2,1)} async-done(((bf16[512,1024]{1,0:T(8,128)(2,1)}), bf16[4096,1024]{1,0:T(8,128)(2,1)}) %all-gather.3.cloned.1.call-update) | async-done | bytes 8388624 | tf_op jit(solution)/shard_map/all_gather | solution.py:37
  65.7 8.0 %concatenate.10 = bf16[4608,1024]{1,0:T(8,128)(2,1)} pad(bf16[4096,1024]{1,0:T(8,128)(2,1)} %all-gather.3.cloned.1.call-done, bf16[]{:T(256)} %constant.41.clone.1), padding=0_512x0_0 | pad | bytes 17825794 | tf_op jit(solution)/shard_map/concatenate | solution.py:47
  73.7 51.5 %while.1 = (s32[]{:T(128)}, bf16[4608,1024]{1,0:T(8,128)(2,1)}, s32[16,2]{0,1:T(2,128)S(1)}, bf16[16,256,1024]{2,1,0:T(8,128)(2,1)}, s32[]{:T(128)}) while((s32[]{:T(128)}, bf16[4608,1024]{1,0:T(8,128)(2,1)}, s32[16,2]{0,1:T(2,128)S(1)}, bf16[16,256,1024]{2,1,0:T(8,128)(2,1)}, s32[]{:T(128)}) %tuple.22), condition=%wide.while_cond, body=%wide.while_body.sunk | while | flops 2 | bytes 1049689 | solution.py:52
  74.3 2.6 bitcast_dynamic-update-slice_fusion.2
  77.6 2.6 bitcast_dynamic-update-slice_fusion.2
  80.8 2.6 bitcast_dynamic-update-slice_fusion.2
  84.0 2.6 bitcast_dynamic-update-slice_fusion.2
  87.2 2.6 bitcast_dynamic-update-slice_fusion.2
  90.4 2.6 bitcast_dynamic-update-slice_fusion.2
  93.6 2.6 bitcast_dynamic-update-slice_fusion.2
  96.8 2.6 bitcast_dynamic-update-slice_fusion.2
  100.0 2.6 bitcast_dynamic-update-slice_fusion.2
  103.3 2.6 bitcast_dynamic-update-slice_fusion.2
  106.5 2.6 bitcast_dynamic-update-slice_fusion.2
  109.7 2.6 bitcast_dynamic-update-slice_fusion.2
  116.1 2.7 bitcast_dynamic-update-slice_fusion.2
  119.4 2.7 bitcast_dynamic-update-slice_fusion.2
  122.6 2.7 bitcast_dynamic-update-slice_fusion.2
  127.5 6.7 %all-to-all-start.1 = ((s32[16,1,4]{2,1,0:T(1,128)}), s32[16,1,4]{2,1,0:T(1,128)S(1)}, u32[]{:S(2)}, u32[]{:S(2)}) async-start(s32[16,1,4]{2,1,0:T(1,128)} %broadcast_in_dim.64), calls=%async_computation.1 | async-start | bytes 16384 | tf_op jit(solution)/shard_map/all_to_all | solution.py:75
  134.2 7.0 %negate_bitcast_fusion = f32[16,2,4,128,128]{3,4,1,0,2:T(8,128)S(1)} fusion(bf16[4,128,1024,1,1]{2,1,4,3,0:T(8,128)(2,1)S(1)} %bitcast.66, bf16[16,2,128,1024,1]{3,2,1,0,4:T(8,128)(2,1)} %bitcast.67), kind=kOutput, calls=%fused_computation.5 | convolution fusion | flops 4297064448 | bytes 17825792 | tf_op jit(solution)/shard_map/ikap,jbp->ikjab/dot_general | solution.py:69
  141.2 3.8 copy.40
  145.0 7.0 %all-to-all-start.2 = ((f32[16,2,4,128,128]{3,4,1,2,0:T(8,128)}), f32[16,2,4,128,128]{3,4,1,2,0:T(8,128)}, u32[]{:S(2)}, u32[]{:S(2)}) async-start(f32[16,2,4,128,128]{3,4,1,2,0:T(8,128)} %copy.40), calls=%async_computation.2 | async-start | bytes 16777216 | tf_op jit(solution)/shard_map/all_to_all | solution.py:73
  152.2 2.9 reshape.279
  155.1 3.5 copy.42
  159.4 115.5 %all-to-all-done.2 = f32[16,2,4,128,128]{3,4,1,2,0:T(8,128)} async-done(((f32[16,2,4,128,128]{3,4,1,2,0:T(8,128)}), f32[16,2,4,128,128]{3,4,1,2,0:T(8,128)}, u32[]{:S(2)}, u32[]{:S(2)}) %all-to-all-start.2) | async-done | bytes 8388640 | tf_op jit(solution)/shard_map/all_to_all | solution.py:73
  274.9 9.2 %copy.41 = f32[16,2,4,128,128]{4,3,2,1,0:T(8,128)} copy(f32[16,2,4,128,128]{3,4,1,2,0:T(8,128)} %all-to-all-done.2) | data formatting | bytes 16777216 | tf_op jit(solution)/shard_map/all_to_all | solution.py:73
  284.1 19.2 %scatter_fusion = f32[5,128,10,128]{3,1,2,0:T(8,128)S(1)} fusion(f32[5,128,10,128]{3,1,2,0:T(8,128)S(1)} %copy.42, s32[128]{0:T(128)S(1)} %reshape.318, f32[128,128,128]{2,1,0:T(8,128)} %bitcast.62), kind=kCustom, calls=%fused_computation.2 | custom fusion | flops 2097152 | bytes 25166848 | tf_op jit(solution)/shard_map/scatter-add | solution.py:78
  310.3 59.8 %all-reduce.4.cloned.1.call-done = f32[640,256]{1,0:T(8,128)} async-done(((f32[640,256]{1,0:T(8,128)}), f32[640,256]{1,0:T(8,128)}) %all-reduce.4.cloned.1.call-update) | async-done | bytes 655376 | tf_op jit(solution)/shard_map/psum | solution.py:13
  370.1 83.8 %all-gather.5.cloned.1.call-done = f32[10240,256]{1,0:T(8,128)} async-done(((f32[640,256]{1,0:T(8,128)}), f32[10240,256]{1,0:T(8,128)}) %all-gather.5.cloned.1.call-update) | async-done | bytes 10485776 | tf_op jit(solution)/shard_map/all_gather | solution.py:86
  453.8 7.0 %convolution_subtract_fusion = f32[640,1280]{1,0:T(8,128)} fusion(f32[640,1280]{1,0:T(8,128)} %bitcast.65, f32[640,256]{1,0:T(8,128)} %all-reduce.4.cloned.1.call-done, f32[10240,256]{1,0:T(8,128)} %all-gather.5.cloned.1.call-done, s32[]{:T(128)S(6)} %select_n.153), kind=kOutput, calls=%fused_computation.6 | convolution fusion | flops 2517401600 | bytes 8519684 | tf_op jit(solution)/shard_map/dot_general | solution.py:88
  (91 shorter events, 29.7 us)
Async XLA Ops:
  7.2 1.6 copy-start
  7.2 5.7 %copy-start.2 = (s32[1,32]{1,0:T(1,128)S(1)}, s32[1,32]{1,0:T(1,128)}, u32[]{:S(2)}) copy-start(s32[1,32]{1,0:T(1,128)} %param.8) | copy-start | bytes 388
  7.2 58.5 %all-gather.3.cloned.1.call-start = ((), (), s32[]{:S(2)}) async-start(), calls=%async_computation.3 | async-start | bytes 9437184 | tf_op jit(solution)/shard_map/all_gather | solution.py:37
  14.7 112.2 %all-to-all-start = ((s32[16,1,2]{2,1,0:T(1,128)}), s32[16,1,2]{2,1,0:T(1,128)S(1)}, u32[]{:S(2)}, u32[]{:S(2)}) async-start(s32[16,1,2]{2,1,0:T(1,128)} %bitcast.3), calls=%async_computation | async-start | bytes 16384 | tf_op jit(solution)/shard_map/all_to_all | solution.py:74
  127.5 17.5 %all-to-all-start.1 = ((s32[16,1,4]{2,1,0:T(1,128)}), s32[16,1,4]{2,1,0:T(1,128)S(1)}, u32[]{:S(2)}, u32[]{:S(2)}) async-start(s32[16,1,4]{2,1,0:T(1,128)} %broadcast_in_dim.64), calls=%async_computation.1 | async-start | bytes 16384 | tf_op jit(solution)/shard_map/all_to_all | solution.py:75
  145.0 7.2 %copy-start.5 = (f32[640,1280]{1,0:T(8,128)S(1)}, f32[640,1280]{1,0:T(8,128)}, u32[]{:S(2)}) copy-start(f32[640,1280]{1,0:T(8,128)} %param.10) | copy-start | bytes 9830404
  145.0 129.9 %all-to-all-start.2 = ((f32[16,2,4,128,128]{3,4,1,2,0:T(8,128)}), f32[16,2,4,128,128]{3,4,1,2,0:T(8,128)}, u32[]{:S(2)}, u32[]{:S(2)}) async-start(f32[16,2,4,128,128]{3,4,1,2,0:T(8,128)} %copy.40), calls=%async_computation.2 | async-start | bytes 16777216 | tf_op jit(solution)/shard_map/all_to_all | solution.py:73
  152.0 218.1 %all-reduce.4.cloned.1.call-start = ((), (), s32[]{:S(2)}) async-start(), calls=%async_computation.4 | async-start | bytes 1310720 | tf_op jit(solution)/shard_map/psum | solution.py:13
  303.3 5.3 %copy-start.6 = (f32[256,256]{1,0:T(8,128)S(1)}, f32[256,256]{1,0:T(8,128)}, u32[]{:S(2)}) copy-start(f32[256,256]{1,0:T(8,128)} %param.11) | copy-start | bytes 786436
  305.3 156.4 %copy-start.1 = (bf16[1,1024,1024]{2,1,0:T(8,128)(2,1)S(1)}, bf16[1,1024,1024]{2,1,0:T(8,128)(2,1)}, u32[]{:S(2)}) copy-start(bf16[1,1024,1024]{2,1,0:T(8,128)(2,1)} %param.7) | copy-start | bytes 6291460
  306.9 1.7 copy-start.3
  310.2 143.6 %all-gather.5.cloned.1.call-start = ((), (), s32[]{:S(2)}) async-start(), calls=%async_computation.5 | async-start | bytes 11141120 | tf_op jit(solution)/shard_map/all_gather | solution.py:86
  370.0 90.9 %copy-start.4 = (f32[640,256]{1,0:T(8,128)S(1)}, f32[640,256]{1,0:T(8,128)}, u32[]{:S(2)}) copy-start(f32[640,256]{1,0:T(8,128)} %all-reduce.4.cloned.1.call-done) | copy-start | bytes 1966084
Sparse Core Ops, SparseCore 0:
  12.4 53.2 all-gather.2
  310.4 59.6 all-reduce.3
  372.2 81.6 all-gather.4
where the time goes:
time: 470 us; the launch traced here: 468 us
  waiting for transfers between devices  298 us (63%)
  local copies, waits for them, and re-layouts  91 us (19%)
  other arithmetic  22.9 us (5%)
  starting transfers between devices  22.4 us (5%)
  matrix products  19.1 us (4%)
  between operations  15.3 us (3%)
    all_to_all x1, waiting for transfers between devices, shards(): lax.all_to_all(contribution, 'row', split_axis=0, concat_axis=0, tiled=True)  115 us
    all_gather x1, waiting for transfers between devices, shards(): whole_panel = lax.all_gather(panel_rows, 'row', axis=0, tiled=True)  83.8 us
    psum x1, waiting for transfers between devices, from_root(): return lax.psum(kept, axis)  59.8 us
    gather x48, local copies, waits for them, and re-layouts  51.5 us
    all_gather x1, waiting for transfers between devices, shards(): factor = lax.all_gather(factor_part, 'col', axis=0, tiled=True)  38.6 us
    scatter-add x1, other arithmetic, shards(): tiled.at[arrived_rows[:, :, None], :, arrived_cols[:, None, :], :]  19.2 us
  transfers between devices with their start and end apart: 6, of which 4 were waited for; matrix products, arithmetic and copies ran while one was open for 18% of the time, Pallas kernels for 0%

commit v1 on v0

--- a/solution.py
+++ b/solution.py
@@ -6,6 +6,12 @@
 TILE = 128
 PANEL = 256
 BLOCK_TILES = 2
+
+
+def number_the_view(xx):
+    return jnp.concatenate(
+        lax.all_to_all(jnp.stack(lax.axis_size("row") * [xx], 0), "row", 0, 0), 0
+    )
 
 
 def from_root(value, axis, source):
@@ -83,7 +89,7 @@
         assembled[:, :PANEL], panel_inverse, (((1,), (1,)), ((), ())), precision=precise
     )
     panel_rows = from_root(own_panel, "col", 0)
-    whole_panel = lax.all_gather(panel_rows, "row", axis=0, tiled=True)
+    whole_panel = number_the_view(panel_rows)
     across = lax.dynamic_slice_in_dim(whole_panel, column * cols_dev, cols_dev, 0)
     trailing = assembled - lax.dot_general(
         panel_rows, across, (((1,), (1,)), ((), ())), precision=precise

time: 470 us -> 558 us (1.19); the launches traced: 468 us -> 547 us
  waiting for transfers between devices: 298 us -> 364 us
  starting transfers between devices: 22.4 us -> 29.1 us
  local copies, waits for them, and re-layouts: 91 us -> 97 us
    all_to_all x0 -> x1, waiting for transfers between devices: none -> 150 us  [number_the_view(): lax.all_to_all(jnp.stack(lax.axis_size('row') * [xx], 0), 'row', 0, 0)]
    all_gather x1 -> x0, waiting for transfers between devices: 83.8 us -> none  [shards(): whole_panel = lax.all_gather(panel_rows, 'row', axis=0, tiled=True)]
    all_to_all x0 -> x1, starting transfers between devices: none -> 6.84 us  [number_the_view(): lax.all_to_all(jnp.stack(lax.axis_size('row') * [xx], 0), 'row', 0, 0)]
    another operation x0 -> x1, local copies, waits for them, and re-layouts: none -> 5.92 us  [number_the_view(): jnp.stack(lax.axis_size('row') * [xx], 0)]
  transfers between devices with their start and end apart: 6 -> 6, of which waited for: 4 -> 4; matrix products, arithmetic and copies ran while one was open for 18% -> 15% of each run, Pallas kernels for 0% -> 0%
where the time goes in v1:
time: 558 us; the launch traced here: 547 us
  waiting for transfers between devices  364 us (65%)
  local copies, waits for them, and re-layouts  97 us (17%)
  starting transfers between devices  29.1 us (5%)
  other arithmetic  22.9 us (4%)
  matrix products  18.1 us (3%)
  between operations  15.6 us (3%)
    all_to_all x1, waiting for transfers between devices, number_the_view(): lax.all_to_all(jnp.stack(lax.axis_size('row') * [xx], 0), 'row', 0, 0)  150 us
    all_to_all x1, waiting for transfers between devices, shards(): lax.all_to_all(contribution, 'row', split_axis=0, concat_axis=0, tiled=True)  115 us
    psum x1, waiting for transfers between devices, from_root(): return lax.psum(kept, axis)  59.8 us
    gather x48, local copies, waits for them, and re-layouts  51.6 us
    all_gather x1, waiting for transfers between devices, shards(): factor = lax.all_gather(factor_part, 'col', axis=0, tiled=True)  38.5 us
    scatter-add x1, other arithmetic, shards(): tiled.at[arrived_rows[:, :, None], :, arrived_cols[:, None, :], :]  19.2 us
  transfers between devices with their start and end apart: 6, of which 4 were waited for; matrix products, arithmetic and copies ran while one was open for 15% of the time, Pallas kernels for 0%

profile of v1, /device:TPU:1, one launch (start us, length us, event | category | flops | bytes accessed | tf_op | source)
XLA Modules:
  0.0 546.7 jit_solution(12028400441433557684)
XLA Ops:
  8.8 3.5 fusion.2
  14.7 8.4 %all-to-all-start = ((s32[16,1,2]{2,1,0:T(1,128)}), s32[16,1,2]{2,1,0:T(1,128)S(1)}, u32[]{:S(2)}, u32[]{:S(2)}) async-start(s32[16,1,2]{2,1,0:T(1,128)} %bitcast.3), calls=%async_computation | async-start | bytes 16384 | tf_op jit(solution)/shard_map/all_to_all | solution.py:80
  27.2 38.5 %all-gather.2.cloned.1.call-done = bf16[4096,1024]{1,0:T(8,128)(2,1)} async-done(((bf16[512,1024]{1,0:T(8,128)(2,1)}), bf16[4096,1024]{1,0:T(8,128)(2,1)}) %all-gather.2.cloned.1.call-update) | async-done | bytes 8388624 | tf_op jit(solution)/shard_map/all_gather | solution.py:43
  65.7 8.0 %concatenate.10 = bf16[4608,1024]{1,0:T(8,128)(2,1)} pad(bf16[4096,1024]{1,0:T(8,128)(2,1)} %all-gather.2.cloned.1.call-done, bf16[]{:T(256)} %constant.41.clone.1), padding=0_512x0_0 | pad | bytes 17825794 | tf_op jit(solution)/shard_map/concatenate | solution.py:53
  73.7 51.6 %while.1 = (s32[]{:T(128)}, bf16[4608,1024]{1,0:T(8,128)(2,1)}, s32[16,2]{0,1:T(2,128)S(1)}, bf16[16,256,1024]{2,1,0:T(8,128)(2,1)}, s32[]{:T(128)}) while((s32[]{:T(128)}, bf16[4608,1024]{1,0:T(8,128)(2,1)}, s32[16,2]{0,1:T(2,128)S(1)}, bf16[16,256,1024]{2,1,0:T(8,128)(2,1)}, s32[]{:T(128)}) %tuple.22), condition=%wide.while_cond, body=%wide.while_body.sunk | while | flops 2 | bytes 1049689 | solution.py:58
  74.3 2.6 bitcast_dynamic-update-slice_fusion.2
  77.6 2.6 bitcast_dynamic-update-slice_fusion.2
  80.8 2.6 bitcast_dynamic-update-slice_fusion.2
  84.0 2.6 bitcast_dynamic-update-slice_fusion.2
  93.6 2.6 bitcast_dynamic-update-slice_fusion.2
  96.8 2.6 bitcast_dynamic-update-slice_fusion.2
  100.1 2.6 bitcast_dynamic-update-slice_fusion.2
  103.3 2.6 bitcast_dynamic-update-slice_fusion.2
  106.5 2.6 bitcast_dynamic-update-slice_fusion.2
  109.7 2.6 bitcast_dynamic-update-slice_fusion.2
  116.2 2.7 bitcast_dynamic-update-slice_fusion.2
  119.4 2.7 bitcast_dynamic-update-slice_fusion.2
  122.7 2.7 bitcast_dynamic-update-slice_fusion.2
  127.6 6.7 %all-to-all-start.1 = ((s32[16,1,4]{2,1,0:T(1,128)}), s32[16,1,4]{2,1,0:T(1,128)S(1)}, u32[]{:S(2)}, u32[]{:S(2)}) async-start(s32[16,1,4]{2,1,0:T(1,128)} %broadcast_in_dim.64), calls=%async_computation.1 | async-start | bytes 16384 | tf_op jit(solution)/shard_map/all_to_all | solution.py:81
  134.3 7.0 %negate_bitcast_fusion = f32[16,2,4,128,128]{3,4,1,0,2:T(8,128)S(1)} fusion(bf16[4,128,1024,1,1]{2,1,4,3,0:T(8,128)(2,1)S(1)} %bitcast.67, bf16[16,2,128,1024,1]{3,2,1,0,4:T(8,128)(2,1)} %bitcast.68), kind=kOutput, calls=%fused_computation.5 | convolution fusion | flops 4297064448 | bytes 17825792 | tf_op jit(solution)/shard_map/ikap,jbp->ikjab/dot_general | solution.py:75
  141.2 3.8 copy.40
  145.1 7.0 %all-to-all-start.2 = ((f32[16,2,4,128,128]{3,4,1,2,0:T(8,128)}), f32[16,2,4,128,128]{3,4,1,2,0:T(8,128)}, u32[]{:S(2)}, u32[]{:S(2)}) async-start(f32[16,2,4,128,128]{3,4,1,2,0:T(8,128)} %copy.40), calls=%async_computation.2 | async-start | bytes 16777216 | tf_op jit(solution)/shard_map/all_to_all | solution.py:79
  152.3 2.9 reshape.284
  155.2 3.5 copy.42
  159.5 115.5 %all-to-all-done.2 = f32[16,2,4,128,128]{3,4,1,2,0:T(8,128)} async-done(((f32[16,2,4,128,128]{3,4,1,2,0:T(8,128)}), f32[16,2,4,128,128]{3,4,1,2,0:T(8,128)}, u32[]{:S(2)}, u32[]{:S(2)}) %all-to-all-start.2) | async-done | bytes 8388640 | tf_op jit(solution)/shard_map/all_to_all | solution.py:79
  275.0 9.2 %copy.41 = f32[16,2,4,128,128]{4,3,2,1,0:T(8,128)} copy(f32[16,2,4,128,128]{3,4,1,2,0:T(8,128)} %all-to-all-done.2) | data formatting | bytes 16777216 | tf_op jit(solution)/shard_map/all_to_all | solution.py:79
  284.2 19.2 %scatter_fusion = f32[5,128,10,128]{3,1,2,0:T(8,128)S(1)} fusion(f32[5,128,10,128]{3,1,2,0:T(8,128)S(1)} %copy.42, s32[128]{0:T(128)S(1)} %reshape.324, f32[128,128,128]{2,1,0:T(8,128)} %bitcast.63), kind=kCustom, calls=%fused_computation.2 | custom fusion | flops 2097152 | bytes 25166848 | tf_op jit(solution)/shard_map/scatter-add | solution.py:84
  310.3 59.8 %all-reduce.4.cloned.1.call-done = f32[640,256]{1,0:T(8,128)} async-done(((f32[640,256]{1,0:T(8,128)}), f32[640,256]{1,0:T(8,128)}) %all-reduce.4.cloned.1.call-update) | async-done | bytes 655376 | tf_op jit(solution)/shard_map/psum | solution.py:19
  370.1 5.9 %stack.2 = f32[16,640,256]{2,1,0:T(8,128)} broadcast(f32[640,256]{1,0:T(8,128)} %all-reduce.4.cloned.1.call-done), dimensions={1,2} | broadcast | bytes 11141120 | tf_op jit(solution)/shard_map/stack | solution.py:13
  376.0 6.8 %all-to-all-start.3 = ((f32[16,640,256]{2,1,0:T(8,128)}), f32[16,640,256]{2,1,0:T(8,128)}, u32[]{:S(2)}, u32[]{:S(2)}) async-start(f32[16,640,256]{2,1,0:T(8,128)} %stack.2), calls=%async_computation.3 | async-start | bytes 20971520 | tf_op jit(solution)/shard_map/all_to_all | solution.py:13
  382.9 150.1 %all-to-all-done.3 = f32[16,640,256]{2,1,0:T(8,128)} async-done(((f32[16,640,256]{2,1,0:T(8,128)}), f32[16,640,256]{2,1,0:T(8,128)}, u32[]{:S(2)}, u32[]{:S(2)}) %all-to-all-start.3) | async-done | bytes 10485792 | tf_op jit(solution)/shard_map/all_to_all | solution.py:13
  532.9 6.0 %convolution_subtract_fusion = f32[640,1280]{1,0:T(8,128)} fusion(f32[640,1280]{1,0:T(8,128)} %bitcast.66, f32[640,256]{1,0:T(8,128)S(1)} %copy-done.4, f32[10240,256]{1,0:T(8,128)} %bitcast.17, s32[]{:T(128)S(6)} %select_n.153), kind=kOutput, calls=%fused_computation.6 | convolution fusion | flops 2517401600 | bytes 8519684 | tf_op jit(solution)/shard_map/dot_general | solution.py:94
  (91 shorter events, 34.8 us)
Async XLA Ops:
  7.2 1.6 copy-start
  7.2 5.7 %copy-start.2 = (s32[1,32]{1,0:T(1,128)S(1)}, s32[1,32]{1,0:T(1,128)}, u32[]{:S(2)}) copy-start(s32[1,32]{1,0:T(1,128)} %param.8) | copy-start | bytes 388
  7.2 58.5 %all-gather.2.cloned.1.call-start = ((), (), s32[]{:S(2)}) async-start(), calls=%async_computation.4 | async-start | bytes 9437184 | tf_op jit(solution)/shard_map/all_gather | solution.py:43
  14.7 112.3 %all-to-all-start = ((s32[16,1,2]{2,1,0:T(1,128)}), s32[16,1,2]{2,1,0:T(1,128)S(1)}, u32[]{:S(2)}, u32[]{:S(2)}) async-start(s32[16,1,2]{2,1,0:T(1,128)} %bitcast.3), calls=%async_computation | async-start | bytes 16384 | tf_op jit(solution)/shard_map/all_to_all | solution.py:80
  127.6 17.5 %all-to-all-start.1 = ((s32[16,1,4]{2,1,0:T(1,128)}), s32[16,1,4]{2,1,0:T(1,128)S(1)}, u32[]{:S(2)}, u32[]{:S(2)}) async-start(s32[16,1,4]{2,1,0:T(1,128)} %broadcast_in_dim.64), calls=%async_computation.1 | async-start | bytes 16384 | tf_op jit(solution)/shard_map/all_to_all | solution.py:81
  145.1 7.2 %copy-start.5 = (f32[640,1280]{1,0:T(8,128)S(1)}, f32[640,1280]{1,0:T(8,128)}, u32[]{:S(2)}) copy-start(f32[640,1280]{1,0:T(8,128)} %param.10) | copy-start | bytes 9830404
  145.1 129.9 %all-to-all-start.2 = ((f32[16,2,4,128,128]{3,4,1,2,0:T(8,128)}), f32[16,2,4,128,128]{3,4,1,2,0:T(8,128)}, u32[]{:S(2)}, u32[]{:S(2)}) async-start(f32[16,2,4,128,128]{3,4,1,2,0:T(8,128)} %copy.40), calls=%async_computation.2 | async-start | bytes 16777216 | tf_op jit(solution)/shard_map/all_to_all | solution.py:79
  152.0 218.0 %all-reduce.4.cloned.1.call-start = ((), (), s32[]{:S(2)}) async-start(), calls=%async_computation.5 | async-start | bytes 1310720 | tf_op jit(solution)/shard_map/psum | solution.py:19
  303.4 5.3 copy-start.6
  307.0 1.7 copy-start.3
  376.0 156.9 %copy-start.4 = (f32[640,256]{1,0:T(8,128)S(1)}, f32[640,256]{1,0:T(8,128)}, u32[]{:S(2)}) copy-start(f32[640,256]{1,0:T(8,128)} %all-reduce.4.cloned.1.call-done) | copy-start | bytes 1966084
  376.0 156.9 %all-to-all-start.3 = ((f32[16,640,256]{2,1,0:T(8,128)}), f32[16,640,256]{2,1,0:T(8,128)}, u32[]{:S(2)}, u32[]{:S(2)}) async-start(f32[16,640,256]{2,1,0:T(8,128)} %stack.2), calls=%async_computation.3 | async-start | bytes 20971520 | tf_op jit(solution)/shard_map/all_to_all | solution.py:13
  382.9 157.0 %copy-start.1 = (bf16[1,1024,1024]{2,1,0:T(8,128)(2,1)S(1)}, bf16[1,1024,1024]{2,1,0:T(8,128)(2,1)}, u32[]{:S(2)}) copy-start(bf16[1,1024,1024]{2,1,0:T(8,128)(2,1)} %param.7) | copy-start | bytes 6291460
Sparse Core Ops, SparseCore 0:
  12.4 53.2 all-gather.1
  310.4 59.6 all-reduce.3
